TPU v7x, 32 devices: a whole 2x2x4 slice. The times are simulated.
32 devices in a mesh: state: 8 (over z, y), mem: 4 (over x, core).
Axes of the slice: x: 2, y: 2, z: 4, core: 2. Of those that a mesh axis runs over, the one named last changes fastest.
Arguments:
- background_matrix: float32 [80, 524288], P('mem', 'state'), may hold values from -6 to 6
- measured_readings: float32 [4, 192], replicated, may hold values from -8 to 8
- measurement_noise: float32 [4, 192], replicated, may hold values from 0.5 to 2
- holding_processor: int32 [4], replicated, may hold values from 0 to 31
- measured_position: int32 [4, 192], replicated, may hold values from 0 to 16383
- taper_grade: int32 [4, 192, 1024], P(None, None, ('state', 'mem')), may hold values from 0 to 4
Outputs:
- analysis: float32 [80, 524288], P(None, ('state', 'mem'))
Inputs may be any that keep to these rules, and one draw needn't show every extreme that they name: `holding_processor`: batches may share an owner; observations of a batch may share a variable.
All inputs are finite; a program needn't handle non-finite values.
Results may differ from a plain program's by a relative error of at most 0.0003.
Values sent between devices are 32-bit elements; how exact they have to be, the bound alone decides.
No kernel may reach another device: no remote copies, remote signals or barrier semaphores. Data moves between devices by JAX's collectives and lax.ppermute only.
A program may use at most 256 MiB of HBM per device.

v0:
```python
import jax
import jax.numpy as jnp
from jax import lax
from jax.sharding import PartitionSpec as P

BATCHES = 4
PRECISE = lax.Precision.HIGHEST


def broadcast(block, axis, source):
    block = jnp.where(lax.axis_index(axis) == source, block, jnp.zeros_like(block))
    return lax.psum(block, axis)


def system_inverse(prior, errors):
    spread = prior - jnp.mean(prior, axis=0)
    system = jnp.dot(spread.T, spread, precision=PRECISE) / (prior.shape[0] - 1) + jnp.diag(errors)
    factor = jnp.linalg.cholesky(system)
    identity = jnp.eye(system.shape[0], dtype=system.dtype)
    lower_inv = lax.linalg.triangular_solve(factor, identity, left_side=True, lower=True)
    return jnp.dot(lower_inv.T, lower_inv, precision=PRECISE)


def expand_levels(levels, block_width):
    scaled = levels.astype(jnp.float32) / 4.0
    widened = scaled[:, :, None] * jnp.ones((block_width,), jnp.float32)
    return widened.reshape(levels.shape[0], levels.shape[1] * block_width)


def update_columns(realization_slab, taper, spread, innovation, inverse):
    center = jnp.mean(realization_slab, axis=0, keepdims=True)
    anomaly = realization_slab - center
    cov = jnp.dot(spread.T, anomaly, precision=PRECISE) / (realization_slab.shape[0] - 1)
    weights = jnp.dot(inverse, taper * cov, precision=PRECISE)
    center = center + jnp.dot(innovation[None, :], weights, precision=PRECISE)
    anomaly = anomaly - 0.5 * jnp.dot(spread, weights, precision=PRECISE)
    return center + anomaly


def announce(prior, root, errors):
    shared = broadcast(prior, ("state", "mem"), root)
    return (shared, system_inverse(shared, errors))


def local(
    background_matrix,
    measured_readings,
    measurement_noise,
    holding_processor,
    measured_position,
    taper_grade,
):
    realization_slab = lax.all_to_all(
        background_matrix, "mem", split_axis=1, concat_axis=0, tiled=True
    )
    block_width = realization_slab.shape[1] // taper_grade.shape[2]
    shared, inverse = announce(
        jnp.take(realization_slab, measured_position[0], axis=1),
        holding_processor[0],
        measurement_noise[0],
    )
    for batch in range(BATCHES):
        center = jnp.mean(shared, axis=0)
        spread = shared - center
        innovation = measured_readings[batch] - center
        taper = expand_levels(taper_grade[batch], block_width)
        if batch + 1 < BATCHES:
            realization_slab = update_columns(realization_slab, taper, spread, innovation, inverse)
            next_prior = jnp.take(realization_slab, measured_position[batch + 1], axis=1)
            shared, inverse = announce(
                next_prior, holding_processor[batch + 1], measurement_noise[batch + 1]
            )
        else:
            realization_slab = update_columns(realization_slab, taper, spread, innovation, inverse)
    return realization_slab


def solution(mesh):
    return jax.shard_map(
        local,
        mesh=mesh,
        in_specs=(P("mem", "state"), P(), P(), P(), P(), P(None, None, ("state", "mem"))),
        out_specs=P(None, ("state", "mem")),
        check_vma=False,
    )
```

profile of v0, /device:TPU:0, one launch (start us, length us, event | category | flops | bytes accessed | tf_op | source)
XLA Modules:
  0.0 761.5 jit_solution(15877180458151621214)
XLA Ops:
  0.0 7.1 all_to_all.14
  7.1 8.1 %copy.24 = f32[20,4,16384]{2,0,1:T(8,128)} copy(f32[20,4,16384]{2,1,0:T(4,128)} %all_to_all.14) | data formatting | bytes 10485760 | tf_op jit(solution)/shard_map/all_to_all | solution.py:53
  15.2 5.5 all-to-all-start
  20.8 4.9 mul.51
  25.7 20.4 %copy.45 = f32[24,8,32,512]{3,1,2,0:T(8,128)} copy(f32[24,8,32,512]{3,2,1,0:T(8,128)} %bitcast.185) | data formatting | bytes 25165824
  46.2 0.7 fusion.127
  48.2 5.3 mul.54
  53.5 20.6 %copy.46 = f32[24,8,32,512]{3,1,2,0:T(8,128)} copy(f32[24,8,32,512]{3,2,1,0:T(8,128)} %bitcast.186) | data formatting | bytes 25165824
  74.8 5.1 mul.57
  79.9 20.4 %copy.47 = f32[24,8,32,512]{3,1,2,0:T(8,128)} copy(f32[24,8,32,512]{3,2,1,0:T(8,128)} %bitcast.187) | data formatting | bytes 25165824
  101.1 5.2 mul.60
  106.3 20.6 %copy.48 = f32[24,8,32,512]{3,1,2,0:T(8,128)} copy(f32[24,8,32,512]{3,2,1,0:T(8,128)} %bitcast.188) | data formatting | bytes 25165824
  127.2 4.6 all_to_all.17
  131.8 7.9 %copy.25 = f32[80,16384]{0,1:T(8,128)} copy(f32[80,16384]{1,0:T(8,128)} %all_to_all.17) | data formatting | bytes 10485760 | tf_op jit(solution)/shard_map/all_to_all | solution.py:53
  139.7 4.1 gather_fusion
  143.9 43.6 %psum.28 = f32[80,192]{0,1:T(8,128)S(1)} all-reduce(f32[80,192]{0,1:T(8,128)S(1)} %bitcast_select_fusion.3), channel_id=1, replica_groups=mesh['state'=8,'mem'=4] {'state','mem'}, use_global_device_ids=true, to_apply=%region_1.3 | all-reduce | flops 15360 | bytes 122880 | tf_op jit(solution)/shard_map/psum | solution.py:12
  188.2 11.7 %cholesky.228 = f32[128,128]{1,0:T(8,128)S(1)} custom-call(f32[128,128]{1,0:T(8,128)S(1)} %cholesky.376), custom_call_target="Cholesky" | custom-call | tf_op jit(solution)/shard_map/jit(cholesky)/cholesky | solution.py:18
  199.9 9.8 %custom-call.17 = f32[1,128,128]{1,2,0:T(8,128)S(1)} custom-call(f32[1,128,128]{2,1,0:T(8,128)S(1)} %get-tuple-element.57), custom_call_target="InvertDiagBlocksLowerTriangular" | custom-call | tf_op jit(solution)/shard_map/jit(cholesky)/cholesky | solution.py:18
  210.1 5.8 cholesky.248
  216.0 0.7 compare_reduce_fusion.7
  216.7 0.7 compare_reduce_fusion.6
  218.8 19.7 %custom-call.18 = f32[2,128,128]{1,2,0:T(8,128)S(1)} custom-call(f32[2,128,128]{2,1,0:T(8,128)S(1)} %pad_maximum_fusion), custom_call_target="InvertDiagBlocksLowerTriangular" | custom-call | tf_op jit(solution)/shard_map/triangular_solve/custom-call.0 | solution.py:20
  239.6 3.2 reduce_sum.70
  242.8 18.8 %fusion.3 = f32[192,16384]{1,0:T(8,128)} fusion(f32[192,16384]{1,0:T(8,128)} %bitcast.192, f32[80,16384]{1,0:T(8,128)} %all_to_all.17, f32[16384]{0:T(1024)S(1)} %broadcast_multiply_fusion.3, f32[80,192]{0,1:T(8,128)S(1)} %psum.28, f32[192]{0:T(256)S(1)} %broadcast_multiply_fusion.7), kind=kOutput, calls=%fused_computation.11 | convolution fusion | flops 3027516416 | bytes 30536448 | tf_op jit(solution)/shard_map/dot_general | solution.py:33
  261.6 15.5 %fusion.131 = f32[192,16384]{1,0:T(8,128)S(1)} fusion(f32[192,192]{1,0:T(8,128)S(1)} %fusion.24, f32[192,16384]{1,0:T(8,128)} %fusion.3), kind=kOutput, calls=%fused_computation.247 | convolution fusion | flops 7247757312 | bytes 25313280 | tf_op jit(solution)/shard_map/dot_general | solution.py:34
  277.2 6.0 fusion.107
  283.2 10.4 %fusion.128 = (f32[16384]{0:T(1024)S(1)}, f32[80,16384]{1,0:T(8,128)}) fusion(f32[192,16384]{1,0:T(8,128)S(1)} %fusion.131, f32[80,192]{0,1:T(8,128)S(1)} %psum.28, f32[192]{0:T(256)S(1)} %broadcast_multiply_fusion.7, f32[80,16384]{1,0:T(8,128)S(1)} %bitcast.184, f32[16384]{0:T(1024)S(1)} %broadcast_multiply_fusion.3, f32[16384]{0:T(1024)S(1)} %fusion.121), kind=kOutput, calls=%fused_computation.244 | convolution fusion | flops 3026451456 | bytes 23327488 | tf_op jit(solution)/shard_map/dot_general | solution.py:36
  293.6 7.9 %copy.29 = f32[80,16384]{0,1:T(8,128)} copy(f32[80,16384]{1,0:T(8,128)} %get-tuple-element.83) | data formatting | bytes 10485760 | tf_op jit(solution)/shard_map/add | solution.py:37
  301.6 4.1 gather_fusion.1
  305.7 41.0 %psum.29 = f32[80,192]{0,1:T(8,128)S(1)} all-reduce(f32[80,192]{0,1:T(8,128)S(1)} %bitcast_select_fusion.2), channel_id=1, replica_groups=mesh['state'=8,'mem'=4] {'state','mem'}, use_global_device_ids=true, to_apply=%region_8.12 | all-reduce | flops 15360 | bytes 122880 | tf_op jit(solution)/shard_map/psum | solution.py:12
  347.4 11.7 %cholesky.266 = f32[128,128]{1,0:T(8,128)S(1)} custom-call(f32[128,128]{1,0:T(8,128)S(1)} %cholesky.379), custom_call_target="Cholesky" | custom-call | tf_op jit(solution)/shard_map/jit(cholesky)/cholesky | solution.py:18
  359.2 9.8 %custom-call.19 = f32[1,128,128]{1,2,0:T(8,128)S(1)} custom-call(f32[1,128,128]{2,1,0:T(8,128)S(1)} %get-tuple-element.55), custom_call_target="InvertDiagBlocksLowerTriangular" | custom-call | tf_op jit(solution)/shard_map/jit(cholesky)/cholesky | solution.py:18
  369.4 5.8 cholesky.286
  375.2 0.7 compare_reduce_fusion.5
  377.9 19.7 %custom-call.20 = f32[2,128,128]{1,2,0:T(8,128)S(1)} custom-call(f32[2,128,128]{2,1,0:T(8,128)S(1)} %pad_maximum_fusion.1), custom_call_target="InvertDiagBlocksLowerTriangular" | custom-call | tf_op jit(solution)/shard_map/triangular_solve/custom-call.0 | solution.py:20
  398.7 18.8 %fusion.2 = f32[192,16384]{1,0:T(8,128)} fusion(f32[192,16384]{1,0:T(8,128)} %bitcast.191, f32[80,16384]{1,0:T(8,128)} %get-tuple-element.83, f32[16384]{0:T(1024)S(1)} %broadcast_multiply_fusion.2, f32[80,192]{0,1:T(8,128)S(1)} %psum.29, f32[192]{0:T(256)S(1)} %broadcast_multiply_fusion.6), kind=kOutput, calls=%fused_computation.9 | convolution fusion | flops 3027516416 | bytes 30536448 | tf_op jit(solution)/shard_map/dot_general | solution.py:33
  417.5 15.5 %fusion.132 = f32[192,16384]{1,0:T(8,128)S(1)} fusion(f32[192,192]{1,0:T(8,128)S(1)} %fusion.28, f32[192,16384]{1,0:T(8,128)} %fusion.2), kind=kOutput, calls=%fused_computation.248 | convolution fusion | flops 7247757312 | bytes 25313280 | tf_op jit(solution)/shard_map/dot_general | solution.py:34
  433.0 6.0 fusion.105
  439.0 10.4 %fusion.129 = (f32[16384]{0:T(1024)S(1)}, f32[80,16384]{1,0:T(8,128)}) fusion(f32[192,16384]{1,0:T(8,128)S(1)} %fusion.132, f32[80,192]{0,1:T(8,128)S(1)} %psum.29, f32[192]{0:T(256)S(1)} %broadcast_multiply_fusion.6, f32[80,16384]{1,0:T(8,128)S(1)} %bitcast.180, f32[16384]{0:T(1024)S(1)} %broadcast_multiply_fusion.2, f32[16384]{0:T(1024)S(1)} %fusion.122), kind=kOutput, calls=%fused_computation.245 | convolution fusion | flops 3026451456 | bytes 23327488 | tf_op jit(solution)/shard_map/dot_general | solution.py:36
  449.5 7.9 %copy.33 = f32[80,16384]{0,1:T(8,128)} copy(f32[80,16384]{1,0:T(8,128)} %get-tuple-element.87) | data formatting | bytes 10485760 | tf_op jit(solution)/shard_map/add | solution.py:37
  457.4 4.1 gather_fusion.2
  461.6 41.0 %psum.30 = f32[80,192]{0,1:T(8,128)S(1)} all-reduce(f32[80,192]{0,1:T(8,128)S(1)} %bitcast_select_fusion.1), channel_id=1, replica_groups=mesh['state'=8,'mem'=4] {'state','mem'}, use_global_device_ids=true, to_apply=%region_11.15 | all-reduce | flops 15360 | bytes 122880 | tf_op jit(solution)/shard_map/psum | solution.py:12
  503.3 11.7 %cholesky.304 = f32[128,128]{1,0:T(8,128)S(1)} custom-call(f32[128,128]{1,0:T(8,128)S(1)} %cholesky.382), custom_call_target="Cholesky" | custom-call | tf_op jit(solution)/shard_map/jit(cholesky)/cholesky | solution.py:18
  515.0 9.8 %custom-call.21 = f32[1,128,128]{1,2,0:T(8,128)S(1)} custom-call(f32[1,128,128]{2,1,0:T(8,128)S(1)} %get-tuple-element.53), custom_call_target="InvertDiagBlocksLowerTriangular" | custom-call | tf_op jit(solution)/shard_map/jit(cholesky)/cholesky | solution.py:18
  525.2 5.8 cholesky.324
  531.1 0.7 compare_reduce_fusion.3
  533.7 19.7 %custom-call.22 = f32[2,128,128]{1,2,0:T(8,128)S(1)} custom-call(f32[2,128,128]{2,1,0:T(8,128)S(1)} %pad_maximum_fusion.2), custom_call_target="InvertDiagBlocksLowerTriangular" | custom-call | tf_op jit(solution)/shard_map/triangular_solve/custom-call.0 | solution.py:20
  554.5 18.9 %fusion.1 = f32[192,16384]{1,0:T(8,128)} fusion(f32[192,16384]{1,0:T(8,128)} %bitcast.190, f32[80,16384]{1,0:T(8,128)} %get-tuple-element.87, f32[16384]{0:T(1024)S(1)} %broadcast_multiply_fusion.1, f32[80,192]{0,1:T(8,128)S(1)} %psum.30, f32[192]{0:T(256)S(1)} %broadcast_multiply_fusion.5), kind=kOutput, calls=%fused_computation.7 | convolution fusion | flops 3027516416 | bytes 30536448 | tf_op jit(solution)/shard_map/dot_general | solution.py:33
  573.5 15.5 %fusion.133 = f32[192,16384]{1,0:T(8,128)S(1)} fusion(f32[192,192]{1,0:T(8,128)S(1)} %fusion.32, f32[192,16384]{1,0:T(8,128)} %fusion.1), kind=kOutput, calls=%fused_computation.249 | convolution fusion | flops 7247757312 | bytes 25313280 | tf_op jit(solution)/shard_map/dot_general | solution.py:34
  589.0 6.0 fusion.103
  595.0 10.4 %fusion.130 = (f32[16384]{0:T(1024)S(1)}, f32[80,16384]{1,0:T(8,128)}) fusion(f32[192,16384]{1,0:T(8,128)S(1)} %fusion.133, f32[80,192]{0,1:T(8,128)S(1)} %psum.30, f32[192]{0:T(256)S(1)} %broadcast_multiply_fusion.5, f32[80,16384]{1,0:T(8,128)S(1)} %bitcast.182, f32[16384]{0:T(1024)S(1)} %broadcast_multiply_fusion.1, f32[16384]{0:T(1024)S(1)} %fusion.123), kind=kOutput, calls=%fused_computation.246 | convolution fusion | flops 3026451456 | bytes 23327488 | tf_op jit(solution)/shard_map/dot_general | solution.py:36
  605.4 7.9 %copy.37 = f32[80,16384]{0,1:T(8,128)} copy(f32[80,16384]{1,0:T(8,128)} %get-tuple-element.91) | data formatting | bytes 10485760 | tf_op jit(solution)/shard_map/add | solution.py:37
  613.4 4.1 gather_fusion.3
  617.5 40.9 %psum.31 = f32[80,192]{0,1:T(8,128)S(1)} all-reduce(f32[80,192]{0,1:T(8,128)S(1)} %bitcast_select_fusion), channel_id=1, replica_groups=mesh['state'=8,'mem'=4] {'state','mem'}, use_global_device_ids=true, to_apply=%region_14.18 | all-reduce | flops 15360 | bytes 122880 | tf_op jit(solution)/shard_map/psum | solution.py:12
  659.2 11.7 %cholesky.342 = f32[128,128]{1,0:T(8,128)S(1)} custom-call(f32[128,128]{1,0:T(8,128)S(1)} %cholesky.385), custom_call_target="Cholesky" | custom-call | tf_op jit(solution)/shard_map/jit(cholesky)/cholesky | solution.py:18
  671.0 9.8 %custom-call.23 = f32[1,128,128]{1,2,0:T(8,128)S(1)} custom-call(f32[1,128,128]{2,1,0:T(8,128)S(1)} %get-tuple-element.51), custom_call_target="InvertDiagBlocksLowerTriangular" | custom-call | tf_op jit(solution)/shard_map/jit(cholesky)/cholesky | solution.py:18
  681.2 5.8 cholesky.362
  687.0 0.7 compare_reduce_fusion.1
  687.7 0.7 compare_reduce_fusion
  689.9 19.7 %custom-call.24 = f32[2,128,128]{1,2,0:T(8,128)S(1)} custom-call(f32[2,128,128]{2,1,0:T(8,128)S(1)} %pad_maximum_fusion.3), custom_call_target="InvertDiagBlocksLowerTriangular" | custom-call | tf_op jit(solution)/shard_map/triangular_solve/custom-call.0 | solution.py:20
  710.6 18.8 %fusion = f32[192,16384]{1,0:T(8,128)} fusion(f32[192,16384]{1,0:T(8,128)} %bitcast.189, f32[80,16384]{1,0:T(8,128)} %get-tuple-element.91, f32[16384]{0:T(1024)S(1)} %broadcast_multiply_fusion, f32[80,192]{0,1:T(8,128)S(1)} %psum.31, f32[192]{0:T(256)S(1)} %broadcast_multiply_fusion.4), kind=kOutput, calls=%fused_computation.5 | convolution fusion | flops 3027516416 | bytes 30536448 | tf_op jit(solution)/shard_map/dot_general | solution.py:33
  729.5 15.4 %fusion.134 = f32[192,16384]{1,0:T(8,128)S(1)} fusion(f32[192,192]{1,0:T(8,128)S(1)} %fusion.36, f32[192,16384]{1,0:T(8,128)} %fusion), kind=kOutput, calls=%fused_computation.250 | convolution fusion | flops 7247757312 | bytes 25313280 | tf_op jit(solution)/shard_map/dot_general | solution.py:34
  744.9 6.0 fusion.101
  750.9 10.2 %fusion.5 = f32[80,16384]{1,0:T(8,128)} fusion(f32[192,16384]{1,0:T(8,128)S(1)} %fusion.134, f32[80,16384]{1,0:T(8,128)S(1)} %bitcast.178, f32[16384]{0:T(1024)S(1)} %fusion.124, f32[16384]{0:T(1024)S(1)} %broadcast_multiply_fusion, f32[80,192]{0,1:T(8,128)S(1)} %psum.31, f32[192]{0:T(256)S(1)} %broadcast_multiply_fusion.4), kind=kOutput, calls=%fused_computation.14 | convolution fusion | flops 3025157120 | bytes 23261952 | tf_op jit(solution)/shard_map/dot_general | solution.py:36
  (145 shorter events, 11.5 us)
Async XLA Ops:
  7.1 13.6 %copy-start = (s32[4,192,32]{1,2,0:T(8,128)S(1)}, s32[4,192,32]{1,2,0:T(8,128)}, u32[]{:S(2)}) copy-start(s32[4,192,32]{1,2,0:T(8,128)} %param.16) | copy-start | bytes 294916
  15.2 111.9 %all-to-all-start = ((f32[20,4,16384]{2,0,1:T(8,128)}), f32[20,4,16384]{2,0,1:T(8,128)}, u32[]{:S(2)}, u32[]{:S(2)}) async-start(f32[20,4,16384]{2,0,1:T(8,128)} %copy.24), calls=%async_computation | async-start | bytes 12582912 | tf_op jit(solution)/shard_map/all_to_all | solution.py:53
  25.7 20.4 %copy-start.2 = (s32[4]{0:T(128)S(1)}, s32[4]{0:T(128)}, u32[]{:S(2)}) copy-start(s32[4]{0:T(128)} %param.14) | copy-start | bytes 52
  106.3 20.6 %copy-start.3 = (s32[4,192]{1,0:T(4,128)S(1)}, s32[4,192]{1,0:T(4,128)}, u32[]{:S(2)}) copy-start(s32[4,192]{1,0:T(4,128)} %param.15) | copy-start | bytes 9220
  106.3 20.8 %copy-start.4 = (f32[4,192]{1,0:T(4,128)S(1)}, f32[4,192]{1,0:T(4,128)}, u32[]{:S(2)}) copy-start(f32[4,192]{1,0:T(4,128)} %param.13) | copy-start | bytes 9220
  261.6 15.5 %copy-start.1 = (f32[4,192]{1,0:T(4,128)S(1)}, f32[4,192]{1,0:T(4,128)}, u32[]{:S(2)}) copy-start(f32[4,192]{1,0:T(4,128)} %param.12) | copy-start | bytes 9220
  277.2 6.0 slice-start.6
  277.2 6.0 slice-start.7
  433.0 6.0 slice-start.2
  433.0 6.0 slice-start.3
  589.0 6.0 slice-start.4
  589.0 6.0 slice-start.5
  744.8 6.0 slice-start
  744.8 6.0 slice-start.1
where the time goes:
time: 767 us; the launch traced here: 761 us
  matrix products  210 us (27%)
  other arithmetic  198 us (26%)
  local copies, waits for them, and re-layouts  172 us (22%)
  blocking collectives  166 us (22%)
  between operations  9.04 us (1%)
    psum x4, blocking collectives, broadcast(): return lax.psum(block, axis)  166 us
    another operation x28, other arithmetic, system_inverse(): factor = jnp.linalg.cholesky(system)  115 us
    unnamed x30, local copies, waits for them, and re-layouts  82.1 us
    another operation x18, other arithmetic, system_inverse(): lax.linalg.triangular_solve(factor, identity, left_side=True, lower=True)  79.2 us
    dot_general x4, matrix products, update_columns(): jnp.dot(spread.T, anomaly, precision=PRECISE)  75.4 us
    dot_general x4, matrix products, update_columns(): weights = jnp.dot(inverse, taper * cov, precision=PRECISE)  61.9 us
    dot_general x4, matrix products, update_columns(): anomaly = anomaly - 0.5 * jnp.dot(spread, weights, precision=PRECISE)  41.4 us
    all_to_all x4, local copies, waits for them, and re-layouts, local(): lax.all_to_all(background_matrix, 'mem', split_axis=1, concat_axis=0, til...  27.8 us
  transfers between devices with their start and end apart: 1, of which 0 were waited for; matrix products, arithmetic and copies ran while one was open for 14% of the time, Pallas kernels for 0%

commit v1 on v0

--- a/solution.py
+++ b/solution.py
@@ -9,7 +9,7 @@
 
 def broadcast(block, axis, source):
     block = jnp.where(lax.axis_index(axis) == source, block, jnp.zeros_like(block))
-    return lax.psum(block, axis)
+    return jnp.sum(lax.all_gather(block, axis), axis=0)
 
 
 def system_inverse(prior, errors):

time: 767 us -> 818 us (1.066)
  waiting for transfers between devices: 0.01 us -> 190 us
  blocking collectives: 166 us -> 0 us
  other arithmetic: 198 us -> 215 us
  between operations: 9.04 us -> 22.3 us
    psum x4 -> x0, blocking collectives: 166 us -> none  [broadcast(): return lax.psum(block, axis)]
    all_gather x0 -> x4, waiting for transfers between devices: none -> 120 us  [broadcast(): return jnp.sum(lax.all_gather(block, axis), axis=0)]
    all_to_all x1, waiting for transfers between devices: 0.01 us -> 69.8 us  [local(): lax.all_to_all(background_matrix, 'mem', split_axis=1, concat_axis=0, til...]
    reduce_sum x4, other arithmetic: 0.41 us -> 8.77 us  [local(): center = jnp.mean(shared, axis=0)]
  transfers between devices with their start and end apart: 1 -> 5, of which waited for: 0 -> 5; matrix products, arithmetic and copies ran while one was open for 14% -> 13% of each run, Pallas kernels for 0% -> 0%
where the time goes in v1:
time: 818 us; the launch traced here: 811 us
  other arithmetic  215 us (26%)
  matrix products  203 us (25%)
  waiting for transfers between devices  190 us (23%)
  local copies, waits for them, and re-layouts  175 us (21%)
  between operations  22.3 us (3%)
    all_gather x4, waiting for transfers between devices, broadcast(): return jnp.sum(lax.all_gather(block, axis), axis=0)  120 us
    another operation x28, other arithmetic, system_inverse(): factor = jnp.linalg.cholesky(system)  115 us
    unnamed x30, local copies, waits for them, and re-layouts  82.6 us
    another operation x18, other arithmetic, system_inverse(): lax.linalg.triangular_solve(factor, identity, left_side=True, lower=True)  79.2 us
    dot_general x4, matrix products, update_columns(): jnp.dot(spread.T, anomaly, precision=PRECISE)  69.9 us
    all_to_all x1, waiting for transfers between devices, local(): lax.all_to_all(background_matrix, 'mem', split_axis=1, concat_axis=0, til...  69.8 us
    dot_general x4, matrix products, update_columns(): weights = jnp.dot(inverse, taper * cov, precision=PRECISE)  61.4 us
    dot_general x4, matrix products, update_columns(): anomaly = anomaly - 0.5 * jnp.dot(spread, weights, precision=PRECISE)  40 us
  transfers between devices with their start and end apart: 5, of which 5 were waited for; matrix products, arithmetic and copies ran while one was open for 13% of the time, Pallas kernels for 0%

profile of v1, /device:TPU:0, one launch (start us, length us, event | category | flops | bytes accessed | tf_op | source)
XLA Modules:
  0.0 810.7 jit_solution(7148612966748265112)
XLA Ops:
  6.5 7.1 all_to_all.14
  13.6 8.2 %copy.45 = f32[20,4,16384]{2,0,1:T(8,128)} copy(f32[20,4,16384]{2,1,0:T(4,128)} %all_to_all.14) | data formatting | bytes 10485760 | tf_op jit(solution)/shard_map/all_to_all | solution.py:53
  21.8 5.4 all-to-all-start
  28.7 69.8 %all-to-all-done = f32[20,4,16384]{2,0,1:T(8,128)} async-done(((f32[20,4,16384]{2,0,1:T(8,128)}), f32[20,4,16384]{2,0,1:T(8,128)}, u32[]{:S(2)}, u32[]{:S(2)}) %all-to-all-start) | async-done | bytes 5242912 | tf_op jit(solution)/shard_map/all_to_all | solution.py:53
  98.5 4.6 all_to_all.17
  103.1 8.0 copy.46
  111.1 4.1 gather_fusion
  116.2 5.0 mul.51
  121.2 20.6 %copy.86 = f32[24,8,32,512]{3,1,2,0:T(8,128)} copy(f32[24,8,32,512]{3,2,1,0:T(8,128)} %bitcast.193) | data formatting | bytes 25165824
  142.6 3.2 reduce_sum.105
  145.8 29.3 %all-gather.9.cloned.1.call-done = f32[2560,192]{1,0:T(8,128)} async-done(((f32[80,192]{1,0:T(8,128)}), f32[2560,192]{1,0:T(8,128)}) %all-gather.9.cloned.1.call-update) | async-done | bytes 1966096 | tf_op jit(solution)/shard_map/all_gather | solution.py:12
  175.0 2.1 reduce_sum.107
  177.2 2.1 reduce_sum.106
  179.8 11.7 %cholesky.228 = f32[128,128]{1,0:T(8,128)S(1)} custom-call(f32[128,128]{1,0:T(8,128)S(1)} %cholesky.376), custom_call_target="Cholesky" | custom-call | tf_op jit(solution)/shard_map/jit(cholesky)/cholesky | solution.py:18
  191.6 9.8 %custom-call.17 = f32[1,128,128]{1,2,0:T(8,128)S(1)} custom-call(f32[1,128,128]{2,1,0:T(8,128)S(1)} %get-tuple-element.57), custom_call_target="InvertDiagBlocksLowerTriangular" | custom-call | tf_op jit(solution)/shard_map/jit(cholesky)/cholesky | solution.py:18
  201.8 5.8 cholesky.248
  210.5 19.7 %custom-call.18 = f32[2,128,128]{1,2,0:T(8,128)S(1)} custom-call(f32[2,128,128]{2,1,0:T(8,128)S(1)} %pad_maximum_fusion), custom_call_target="InvertDiagBlocksLowerTriangular" | custom-call | tf_op jit(solution)/shard_map/triangular_solve/custom-call.0 | solution.py:20
  231.2 17.6 %fusion.3 = f32[192,16384]{1,0:T(8,128)} fusion(f32[192,16384]{1,0:T(8,128)} %bitcast.189, f32[80,16384]{1,0:T(8,128)} %all_to_all.17, f32[16384]{0:T(1024)S(1)} %broadcast_multiply_fusion.3, f32[80,192]{1,0:T(8,128)S(1)} %reduce_sum.107, f32[192]{0:T(256)S(1)} %broadcast_multiply_fusion.7), kind=kOutput, calls=%fused_computation.11 | convolution fusion | flops 3027516416 | bytes 30536448 | tf_op jit(solution)/shard_map/dot_general | solution.py:33
  248.8 15.3 %fusion.131 = f32[192,16384]{1,0:T(8,128)S(1)} fusion(f32[192,192]{1,0:T(8,128)S(1)} %fusion.24, f32[192,16384]{1,0:T(8,128)} %fusion.3), kind=kOutput, calls=%fused_computation.247 | convolution fusion | flops 7247757312 | bytes 25313280 | tf_op jit(solution)/shard_map/dot_general | solution.py:34
  264.2 6.0 fusion.107
  270.2 10.1 %fusion.128 = (f32[16384]{0:T(1024)S(1)}, f32[80,16384]{1,0:T(8,128)}) fusion(f32[192,16384]{1,0:T(8,128)S(1)} %fusion.131, f32[80,192]{1,0:T(8,128)S(1)} %reduce_sum.107, f32[192]{0:T(256)S(1)} %broadcast_multiply_fusion.7, f32[80,16384]{1,0:T(8,128)S(1)} %bitcast.182, f32[16384]{0:T(1024)S(1)} %broadcast_multiply_fusion.3, f32[16384]{0:T(1024)S(1)} %fusion.121), kind=kOutput, calls=%fused_computation.244 | convolution fusion | flops 3026451456 | bytes 23327488 | tf_op jit(solution)/shard_map/dot_general | solution.py:36
  280.3 7.9 copy.53
  288.2 4.1 gather_fusion.1
  293.3 5.0 mul.54
  298.3 20.6 %copy.87 = f32[24,8,32,512]{3,1,2,0:T(8,128)} copy(f32[24,8,32,512]{3,2,1,0:T(8,128)} %bitcast.194) | data formatting | bytes 25165824
  319.7 30.0 %all-gather.11.cloned.1.call-done = f32[2560,192]{1,0:T(8,128)} async-done(((f32[80,192]{1,0:T(8,128)}), f32[2560,192]{1,0:T(8,128)}) %all-gather.11.cloned.1.call-update) | async-done | bytes 1966096 | tf_op jit(solution)/shard_map/all_gather | solution.py:12
  349.7 1.9 reduce_sum.129
  351.6 2.5 reduce_sum.128
  354.7 11.7 %cholesky.266 = f32[128,128]{1,0:T(8,128)S(1)} custom-call(f32[128,128]{1,0:T(8,128)S(1)} %cholesky.379), custom_call_target="Cholesky" | custom-call | tf_op jit(solution)/shard_map/jit(cholesky)/cholesky | solution.py:18
  366.4 9.8 %custom-call.19 = f32[1,128,128]{1,2,0:T(8,128)S(1)} custom-call(f32[1,128,128]{2,1,0:T(8,128)S(1)} %get-tuple-element.55), custom_call_target="InvertDiagBlocksLowerTriangular" | custom-call | tf_op jit(solution)/shard_map/jit(cholesky)/cholesky | solution.py:18
  376.6 5.8 cholesky.286
  385.3 19.7 %custom-call.20 = f32[2,128,128]{1,2,0:T(8,128)S(1)} custom-call(f32[2,128,128]{2,1,0:T(8,128)S(1)} %pad_maximum_fusion.1), custom_call_target="InvertDiagBlocksLowerTriangular" | custom-call | tf_op jit(solution)/shard_map/triangular_solve/custom-call.0 | solution.py:20
  406.1 17.4 %fusion.2 = f32[192,16384]{1,0:T(8,128)} fusion(f32[192,16384]{1,0:T(8,128)} %bitcast.190, f32[80,16384]{1,0:T(8,128)} %get-tuple-element.83, f32[16384]{0:T(1024)S(1)} %broadcast_multiply_fusion.2, f32[80,192]{1,0:T(8,128)S(1)} %reduce_sum.129, f32[192]{0:T(256)S(1)} %broadcast_multiply_fusion.6), kind=kOutput, calls=%fused_computation.9 | convolution fusion | flops 3027516416 | bytes 30536448 | tf_op jit(solution)/shard_map/dot_general | solution.py:33
  423.5 15.3 %fusion.132 = f32[192,16384]{1,0:T(8,128)S(1)} fusion(f32[192,192]{1,0:T(8,128)S(1)} %fusion.28, f32[192,16384]{1,0:T(8,128)} %fusion.2), kind=kOutput, calls=%fused_computation.248 | convolution fusion | flops 7247757312 | bytes 25313280 | tf_op jit(solution)/shard_map/dot_general | solution.py:34
  438.8 6.0 fusion.105
  444.8 10.1 %fusion.129 = (f32[16384]{0:T(1024)S(1)}, f32[80,16384]{1,0:T(8,128)}) fusion(f32[192,16384]{1,0:T(8,128)S(1)} %fusion.132, f32[80,192]{1,0:T(8,128)S(1)} %reduce_sum.129, f32[192]{0:T(256)S(1)} %broadcast_multiply_fusion.6, f32[80,16384]{1,0:T(8,128)S(1)} %bitcast.184, f32[16384]{0:T(1024)S(1)} %broadcast_multiply_fusion.2, f32[16384]{0:T(1024)S(1)} %fusion.122), kind=kOutput, calls=%fused_computation.245 | convolution fusion | flops 3026451456 | bytes 23327488 | tf_op jit(solution)/shard_map/dot_general | solution.py:36
  454.9 7.9 copy.60
  462.8 4.1 gather_fusion.2
  467.9 5.2 mul.57
  473.1 20.6 %copy.88 = f32[24,8,32,512]{3,1,2,0:T(8,128)} copy(f32[24,8,32,512]{3,2,1,0:T(8,128)} %bitcast.195) | data formatting | bytes 25165824
  494.5 29.9 %all-gather.13.cloned.1.call-done = f32[2560,192]{1,0:T(8,128)} async-done(((f32[80,192]{1,0:T(8,128)}), f32[2560,192]{1,0:T(8,128)}) %all-gather.13.cloned.1.call-update) | async-done | bytes 1966096 | tf_op jit(solution)/shard_map/all_gather | solution.py:12
  526.3 2.1 reduce_sum.131
  529.1 11.7 %cholesky.304 = f32[128,128]{1,0:T(8,128)S(1)} custom-call(f32[128,128]{1,0:T(8,128)S(1)} %cholesky.382), custom_call_target="Cholesky" | custom-call | tf_op jit(solution)/shard_map/jit(cholesky)/cholesky | solution.py:18
  540.9 9.8 %custom-call.21 = f32[1,128,128]{1,2,0:T(8,128)S(1)} custom-call(f32[1,128,128]{2,1,0:T(8,128)S(1)} %get-tuple-element.53), custom_call_target="InvertDiagBlocksLowerTriangular" | custom-call | tf_op jit(solution)/shard_map/jit(cholesky)/cholesky | solution.py:18
  551.1 5.8 cholesky.324
  559.8 19.7 %custom-call.22 = f32[2,128,128]{1,2,0:T(8,128)S(1)} custom-call(f32[2,128,128]{2,1,0:T(8,128)S(1)} %pad_maximum_fusion.2), custom_call_target="InvertDiagBlocksLowerTriangular" | custom-call | tf_op jit(solution)/shard_map/triangular_solve/custom-call.0 | solution.py:20
  580.5 17.4 %fusion.1 = f32[192,16384]{1,0:T(8,128)} fusion(f32[192,16384]{1,0:T(8,128)} %bitcast.191, f32[80,16384]{1,0:T(8,128)} %get-tuple-element.87, f32[16384]{0:T(1024)S(1)} %broadcast_multiply_fusion.1, f32[80,192]{1,0:T(8,128)S(1)} %reduce_sum.132, f32[192]{0:T(256)S(1)} %broadcast_multiply_fusion.5), kind=kOutput, calls=%fused_computation.7 | convolution fusion | flops 3027516416 | bytes 30536448 | tf_op jit(solution)/shard_map/dot_general | solution.py:33
  597.9 15.5 %fusion.133 = f32[192,16384]{1,0:T(8,128)S(1)} fusion(f32[192,192]{1,0:T(8,128)S(1)} %fusion.32, f32[192,16384]{1,0:T(8,128)} %fusion.1), kind=kOutput, calls=%fused_computation.249 | convolution fusion | flops 7247757312 | bytes 25313280 | tf_op jit(solution)/shard_map/dot_general | solution.py:34
  613.5 6.0 fusion.103
  619.5 10.1 %fusion.130 = (f32[16384]{0:T(1024)S(1)}, f32[80,16384]{1,0:T(8,128)}) fusion(f32[192,16384]{1,0:T(8,128)S(1)} %fusion.133, f32[80,192]{1,0:T(8,128)S(1)} %reduce_sum.132, f32[192]{0:T(256)S(1)} %broadcast_multiply_fusion.5, f32[80,16384]{1,0:T(8,128)S(1)} %bitcast.186, f32[16384]{0:T(1024)S(1)} %broadcast_multiply_fusion.1, f32[16384]{0:T(1024)S(1)} %fusion.123), kind=kOutput, calls=%fused_computation.246 | convolution fusion | flops 3026451456 | bytes 23327488 | tf_op jit(solution)/shard_map/dot_general | solution.py:36
  629.6 7.9 copy.67
  637.5 4.1 gather_fusion.3
  642.5 5.0 mul.60
  647.5 20.6 %copy.89 = f32[24,8,32,512]{3,1,2,0:T(8,128)} copy(f32[24,8,32,512]{3,2,1,0:T(8,128)} %bitcast.196) | data formatting | bytes 25165824
  668.2 30.8 %all-gather.15.cloned.1.call-done = f32[2560,192]{1,0:T(8,128)} async-done(((f32[80,192]{1,0:T(8,128)}), f32[2560,192]{1,0:T(8,128)}) %all-gather.15.cloned.1.call-update) | async-done | bytes 1966096 | tf_op jit(solution)/shard_map/all_gather | solution.py:12
  700.9 2.1 reduce_sum.134
  703.8 11.7 %cholesky.342 = f32[128,128]{1,0:T(8,128)S(1)} custom-call(f32[128,128]{1,0:T(8,128)S(1)} %cholesky.385), custom_call_target="Cholesky" | custom-call | tf_op jit(solution)/shard_map/jit(cholesky)/cholesky | solution.py:18
  715.5 9.8 %custom-call.23 = f32[1,128,128]{1,2,0:T(8,128)S(1)} custom-call(f32[1,128,128]{2,1,0:T(8,128)S(1)} %get-tuple-element.51), custom_call_target="InvertDiagBlocksLowerTriangular" | custom-call | tf_op jit(solution)/shard_map/jit(cholesky)/cholesky | solution.py:18
  725.7 5.8 cholesky.362
  734.4 19.7 %custom-call.24 = f32[2,128,128]{1,2,0:T(8,128)S(1)} custom-call(f32[2,128,128]{2,1,0:T(8,128)S(1)} %pad_maximum_fusion.3), custom_call_target="InvertDiagBlocksLowerTriangular" | custom-call | tf_op jit(solution)/shard_map/triangular_solve/custom-call.0 | solution.py:20
  755.2 17.6 %fusion = f32[192,16384]{1,0:T(8,128)} fusion(f32[192,16384]{1,0:T(8,128)} %bitcast.192, f32[80,16384]{1,0:T(8,128)} %get-tuple-element.91, f32[16384]{0:T(1024)S(1)} %broadcast_multiply_fusion, f32[80,192]{1,0:T(8,128)S(1)} %reduce_sum.135, f32[192]{0:T(256)S(1)} %broadcast_multiply_fusion.4), kind=kOutput, calls=%fused_computation.5 | convolution fusion | flops 3027516416 | bytes 30536448 | tf_op jit(solution)/shard_map/dot_general | solution.py:33
  772.8 15.3 %fusion.134 = f32[192,16384]{1,0:T(8,128)S(1)} fusion(f32[192,192]{1,0:T(8,128)S(1)} %fusion.36, f32[192,16384]{1,0:T(8,128)} %fusion), kind=kOutput, calls=%fused_computation.250 | convolution fusion | flops 7247757312 | bytes 25313280 | tf_op jit(solution)/shard_map/dot_general | solution.py:34
  788.1 6.0 fusion.101
  794.1 9.8 %fusion.5 = f32[80,16384]{1,0:T(8,128)} fusion(f32[192,16384]{1,0:T(8,128)S(1)} %fusion.134, f32[80,16384]{1,0:T(8,128)S(1)} %bitcast.188, f32[16384]{0:T(1024)S(1)} %fusion.124, f32[16384]{0:T(1024)S(1)} %broadcast_multiply_fusion, f32[80,192]{1,0:T(8,128)S(1)} %reduce_sum.135, f32[192]{0:T(256)S(1)} %broadcast_multiply_fusion.4), kind=kOutput, calls=%fused_computation.14 | convolution fusion | flops 3025157120 | bytes 23261952 | tf_op jit(solution)/shard_map/dot_general | solution.py:36
  (160 shorter events, 23.0 us)
Async XLA Ops:
  21.8 5.5 copy-start.2
  21.8 6.9 copy-start.3
  21.8 76.7 %all-to-all-start = ((f32[20,4,16384]{2,0,1:T(8,128)}), f32[20,4,16384]{2,0,1:T(8,128)}, u32[]{:S(2)}, u32[]{:S(2)}) async-start(f32[20,4,16384]{2,0,1:T(8,128)} %copy.45), calls=%async_computation | async-start | bytes 12582912 | tf_op jit(solution)/shard_map/all_to_all | solution.py:53
  27.3 147.8 %all-gather.9.cloned.1.call-start = ((), (), s32[]{:S(2)}) async-start(), calls=%async_computation.1 | async-start | bytes 2703360 | tf_op jit(solution)/shard_map/all_gather | solution.py:12
  103.1 12.9 %copy-start = (s32[4,192,32]{1,2,0:T(8,128)S(1)}, s32[4,192,32]{1,2,0:T(8,128)}, u32[]{:S(2)}) copy-start(s32[4,192,32]{1,2,0:T(8,128)} %param.16) | copy-start | bytes 294916
  116.0 233.7 %all-gather.11.cloned.1.call-start = ((), (), s32[]{:S(2)}) async-start(), calls=%async_computation.2 | async-start | bytes 2703360 | tf_op jit(solution)/shard_map/all_gather | solution.py:12
  121.2 21.3 %copy-start.4 = (f32[4,192]{1,0:T(4,128)S(1)}, f32[4,192]{1,0:T(4,128)}, u32[]{:S(2)}) copy-start(f32[4,192]{1,0:T(4,128)} %param.13) | copy-start | bytes 9220
  248.8 15.3 %copy-start.1 = (f32[4,192]{1,0:T(4,128)S(1)}, f32[4,192]{1,0:T(4,128)}, u32[]{:S(2)}) copy-start(f32[4,192]{1,0:T(4,128)} %param.12) | copy-start | bytes 9220
  264.1 6.0 slice-start
  264.1 6.0 slice-start.1
  293.1 231.3 %all-gather.13.cloned.1.call-start = ((), (), s32[]{:S(2)}) async-start(), calls=%async_computation.3 | async-start | bytes 2703360 | tf_op jit(solution)/shard_map/all_gather | solution.py:12
  438.8 6.0 slice-start.2
  438.8 6.0 slice-start.3
  467.8 231.3 %all-gather.15.cloned.1.call-start = ((), (), s32[]{:S(2)}) async-start(), calls=%async_computation.4 | async-start | bytes 2703360 | tf_op jit(solution)/shard_map/all_gather | solution.py:12
  613.4 6.0 slice-start.4
  613.5 6.0 slice-start.5
  788.1 6.0 slice-start.6
  788.1 6.0 slice-start.7
Sparse Core Ops, SparseCore 0:
  116.2 58.8 all-gather.8
  293.2 56.4 all-gather.10
  467.9 56.4 all-gather.12
  642.5 56.4 all-gather.14
